TPU v7x, 256 devices: a whole 4x4x8 slice. The times are simulated.
256 devices in a mesh: tm: 32 (over y, z), space: 8 (over x, core).
Axes of the slice: x: 4, y: 4, z: 8, core: 2. Of those that a mesh axis runs over, the one named last changes fastest.
Arguments:
- inverse_factor: bfloat16 [2, 32, 4096, 4096], P(None, 'tm', 'space'), may hold values from -1.5 to 1.5, as said below
- tile_mask: int32 [32, 32], replicated, may hold values 0 or 1
- carry_rate: float32 [32, 4096, 2], P('tm', 'space'), may hold values from 0 to 1
- right_side: float32 [32, 4096, 2, 128], P('tm', 'space'), may hold values from -1.5 to 1.5
- arrow_rows: bfloat16 [32, 4096, 2, 512], P('tm', 'space'), may hold values from -0.0625 to 0.0625
- fixed_rhs: float32 [2, 512, 128], P(None, ('tm', 'space')), may hold values from -6 to 6
- tip_factor: bfloat16 [2, 512, 512], replicated, may hold values from -1 to 1, as said below
Outputs:
- solution: float32 [32, 4096, 2, 128], P('tm', 'space')
- fixed_solution: float32 [2, 512, 128], P(None, ('tm', 'space'))
Inputs may be any that keep to these rules, and one draw needn't show every extreme that they name: `tile_mask`: 1 marks a tile that may be nonzero. `inverse_factor`: only entries on or below the diagonal are read. `tip_factor`: only entries on or below the diagonal are read.
All inputs are finite; a program needn't handle non-finite values.
Results may differ from a plain program's by a relative error of at most 0.022.
Values may be sent and summed in bfloat16 or wider, within the bound.
No kernel may reach another device: no remote copies, remote signals or barrier semaphores. Data moves between devices by JAX's collectives and lax.ppermute only.
A program may use at most 320 MiB of HBM per device.

v0:
```python
import jax
import jax.numpy as jnp
from jax import lax
from jax.sharding import PartitionSpec as P

TILE = 128


def carried_in(shard, axis, join, neutral, backward):
    count = lax.axis_size(axis)
    place = lax.axis_index(axis)
    ahead = count - 1 - place if backward else place
    gathered = jax.tree.map(
        lambda a, kind: lax.all_gather(a.astype(kind), axis), shard, (jnp.bfloat16, jnp.bfloat16)
    )
    state = jax.tree.map(lambda a, e: jnp.zeros_like(a) + jnp.asarray(e, a.dtype), shard, neutral)

    def one(turn, state):
        source = count - 1 - turn if backward else turn
        return join(
            state,
            jax.tree.map(
                lambda a, own: lax.dynamic_index_in_dim(a, source, 0, False).astype(own.dtype),
                gathered,
                shard,
            ),
        )

    return lax.fori_loop(0, ahead, one, state)


def combine(earlier, latter):
    rate_new = latter[0] * earlier[0]
    rest = tuple(
        (value_l + latter[0] * value_e for value_l, value_e in zip(latter[1:], earlier[1:]))
    )
    return (rate_new,) + rest


def tile_keep(tile_table, row_start, row_total, col_total):
    tile_count = tile_table.shape[0]
    tile_ids = jnp.arange(tile_count, dtype=jnp.int32)
    row_index = row_start + jnp.arange(row_total, dtype=jnp.int32)
    col_index = jnp.arange(col_total, dtype=jnp.int32)
    row_onehot = (row_index[:, None] // TILE == tile_ids[None, :]).astype(jnp.float32)
    col_onehot = (col_index[:, None] // TILE == tile_ids[None, :]).astype(jnp.float32)
    marked = jnp.dot(jnp.dot(row_onehot, tile_table.astype(jnp.float32)), col_onehot.T)
    return (marked > 0.5) & (row_index[:, None] >= col_index[None, :])


def on_device(inverse_factor, tile_mask, carry_rate, right_side, arrow_rows, fixed_rhs, tip_factor):
    row_count = right_side.shape[1]
    node_total = inverse_factor.shape[3]
    row_start = lax.axis_index("space") * row_count
    tile_table = jnp.maximum(tile_mask, jnp.eye(tile_mask.shape[0], dtype=jnp.int32))
    weights = inverse_factor[:, 0]
    bf_zero = jnp.zeros((), jnp.bfloat16)
    rate_col = carry_rate[0][:, :, None]
    source = right_side[0]
    unit_rate = jnp.ones_like(rate_col)
    earlier_sum = carried_in(
        (rate_col, source), "tm", combine, (unit_rate, jnp.zeros_like(source)), False
    )
    forward = source + rate_col * earlier_sum[1]
    forward_b = forward.astype(jnp.bfloat16)
    row_keep = tile_keep(tile_table, row_start, row_count, node_total)
    masked_rows = jnp.where(row_keep[None], weights, bf_zero)
    block = masked_rows
    inner_rows = jnp.einsum(
        "hrn,nhk->rhk",
        block,
        lax.all_gather(forward_b, "space", axis=0, tiled=True),
        preferred_element_type=jnp.float32,
    ).astype(jnp.bfloat16)
    block = masked_rows
    scaled = lax.psum_scatter(
        jnp.einsum("hrn,rhk->nhk", block, inner_rows, preferred_element_type=jnp.float32).astype(
            jnp.bfloat16
        ),
        "space",
        scatter_dimension=0,
        tiled=True,
    ).astype(jnp.float32)
    arrow_part = arrow_rows[0]
    coupling = jnp.einsum("rhf,rhk->hfk", arrow_part, forward_b, preferred_element_type=jnp.float32)
    share_rows = fixed_rhs.shape[1]
    share_start = lax.axis_index(("tm", "space")) * share_rows
    contrib = -coupling
    own_part = lax.dynamic_slice_in_dim(contrib, share_start, share_rows, 1) + fixed_rhs
    contrib = lax.dynamic_update_slice_in_dim(contrib, own_part, share_start, 1)
    fixed_forward = lax.psum(contrib, ("tm", "space")).astype(jnp.bfloat16)
    fixed_total = tip_factor.shape[1]
    fixed_index = jnp.arange(fixed_total, dtype=jnp.int32)
    lower_tri = fixed_index[:, None] >= fixed_index[None, :]
    tip_lower = jnp.where(lower_tri[None], tip_factor, bf_zero)
    tip_inner = jnp.einsum(
        "hij,hjk->hik", tip_lower, fixed_forward, preferred_element_type=jnp.float32
    ).astype(jnp.bfloat16)
    fixed_solution = jnp.einsum(
        "hij,hik->hjk", tip_lower, tip_inner, preferred_element_type=jnp.float32
    )
    fixed_own = lax.dynamic_slice_in_dim(fixed_solution, share_start, share_rows, 1)
    fixed_b = fixed_solution.astype(jnp.bfloat16)
    carried = scaled - jnp.einsum(
        "rhf,hfk->rhk", arrow_part, fixed_b, preferred_element_type=jnp.float32
    )
    following = carried_in(
        (rate_col, rate_col * carried), "tm", combine, (unit_rate, jnp.zeros_like(carried)), True
    )
    solution = carried + following[1]
    return (solution[None], fixed_own)


def solution(mesh):
    placed = (
        P(None, "tm", "space", None),
        P(),
        P("tm", "space", None),
        P("tm", "space", None, None),
        P("tm", "space", None, None),
        P(None, ("tm", "space"), None),
        P(),
    )
    return jax.shard_map(
        on_device,
        mesh=mesh,
        in_specs=placed,
        out_specs=(P("tm", "space", None, None), P(None, ("tm", "space"), None)),
        check_vma=False,
    )
```

profile of v0, /device:TPU:2, one launch (start us, length us, event | category | flops | bytes accessed | tf_op | source)
XLA Modules:
  0.0 596.0 jit_solution(12626880782622736189)
XLA Ops:
  7.2 1.9 copy.62
  9.2 1.2 copy.34
  11.1 52.1 %all-gather = bf16[32,512,2]{1,2,0:T(2,128)(2,1)S(1)} all-gather(bf16[1,512,2]{1,2,0:T(2,128)(2,1)S(1)} %convert_element_type.103), channel_id=2, replica_groups=mesh['tm'=32,'space'=8] {'tm'}, dimensions={0}, use_global_device_ids=true | all-gather | bytes 67584 | tf_op jit(solution)/shard_map/all_gather | solution.py:14
  63.2 3.3 copy.37
  66.6 46.1 %all-gather.6.cloned.1.call-done = bf16[32,512,2,128]{3,1,2,0:T(8,128)(2,1)} async-done(((bf16[1,512,2,128]{3,1,2,0:T(8,128)(2,1)}), bf16[32,512,2,128]{3,1,2,0:T(8,128)(2,1)}) %all-gather.6.cloned.1.call-update) | async-done | bytes 8388624 | tf_op jit(solution)/shard_map/all_gather | solution.py:14
  114.4 4.2 fusion
  118.6 154.2 %all-gather.8.cloned.1.call-done = bf16[4096,2,128]{0,2,1:T(8,128)(2,1)} async-done(((bf16[512,2,128]{0,2,1:T(8,128)(2,1)}), bf16[4096,2,128]{0,2,1:T(8,128)(2,1)}) %all-gather.8.cloned.1.call-update) | async-done | bytes 2097168 | tf_op jit(solution)/shard_map/all_gather | solution.py:72
  272.7 13.2 %fusion.4 = bf16[4096,2,128]{0,2,1:T(8,128)(2,1)} fusion(bf16[2,1,512,4096]{3,2,1,0:T(8,128)(2,1)} %param.11, pred[512,4096]{1,0:T(8,128)(4,1)} %fusion, bf16[4096,2,128]{0,2,1:T(8,128)(2,1)} %all-gather.8.cloned.1.call-done), kind=kOutput, calls=%fused_computation.12 | convolution fusion | flops 2157051904 | bytes 14680064 | tf_op jit(solution)/shard_map/hrn,rhk->nhk/dot_general | solution.py:77
  286.7 1.1 dynamic_update_slice.3
  287.8 78.9 %all-reduce.1 = bf16[2,512,128]{1,2,0:T(8,128)(2,1)S(1)} all-reduce(f32[2,512,128]{1,2,0:T(8,128)S(1)} %dynamic_update_slice.3), channel_id=1, replica_groups=mesh['tm'=32,'space'=8] {'tm','space'}, use_global_device_ids=true, to_apply=%region_3.4 | all-reduce | flops 131072 | bytes 786432 | tf_op jit(solution)/shard_map/psum | solution.py:91
  366.7 2.3 fusion.9
  369.0 2.1 multiply_convert_fusion
  371.8 102.9 %all-gather.10.cloned.1.call-done = bf16[16384,2,128]{0,2,1:T(8,128)(2,1)} async-done(((bf16[512,2,128]{0,2,1:T(8,128)(2,1)}), bf16[16384,2,128]{0,2,1:T(8,128)(2,1)}) %all-gather.10.cloned.1.call-update) | async-done | bytes 8388624 | tf_op jit(solution)/shard_map/all_gather | solution.py:14
  474.7 21.1 %copy.52 = bf16[16384,2,128]{2,1,0:T(2,128)(2,1)} copy(bf16[16384,2,128]{0,2,1:T(8,128)(2,1)} %all-gather.10.cloned.1.call-done) | data formatting | bytes 16777216 | tf_op jit(solution)/shard_map/while | solution.py:29
  495.9 92.2 %while.27 = (s32[]{:T(128)}, f32[512,2,128]{2,1,0:T(2,128)S(1)}, s32[]{:T(128)}, bf16[32,512,2,128]{3,2,1,0:T(2,128)(2,1)}, bf16[32,512,2,1]{2,1,3,0:T(8,128)(2,...) while((s32[]{:T(128)}, f32[512,2,128]{2,1,0:T(2,128)S(1)}, s32[]{:T(128)}, ...), condition=%wide.region_5.6_spmd, body=%wide.region_4.5_spmd.sunk | while | flops 394246 | bytes 1321107 | solution.py:29
  495.9 0.9 bitcast_convert_fusion.5
  496.9 2.0 convert_add_fusion.5
  499.8 2.0 convert_add_fusion.5
  502.8 2.0 convert_add_fusion.5
  505.8 2.0 convert_add_fusion.5
  508.8 2.0 convert_add_fusion.5
  511.7 2.0 convert_add_fusion.5
  514.7 2.0 convert_add_fusion.5
  517.7 2.0 convert_add_fusion.5
  520.7 2.0 convert_add_fusion.5
  523.6 2.0 convert_add_fusion.5
  526.6 2.0 convert_add_fusion.5
  529.6 2.0 convert_add_fusion.5
  532.6 2.0 convert_add_fusion.5
  535.5 2.0 convert_add_fusion.5
  538.5 2.0 convert_add_fusion.5
  541.5 2.0 convert_add_fusion.5
  544.5 2.0 convert_add_fusion.5
  547.4 2.0 convert_add_fusion.5
  550.4 2.0 convert_add_fusion.5
  553.4 2.0 convert_add_fusion.5
  556.3 2.0 convert_add_fusion.5
  559.3 2.0 convert_add_fusion.5
  562.3 2.0 convert_add_fusion.5
  565.3 2.0 convert_add_fusion.5
  568.2 2.0 convert_add_fusion.5
  571.2 2.0 convert_add_fusion.5
  574.2 2.0 convert_add_fusion.5
  577.2 2.0 convert_add_fusion.5
  580.1 2.0 convert_add_fusion.5
  583.1 2.0 convert_add_fusion.5
  586.1 2.0 convert_add_fusion.5
  588.4 1.0 copy.48
  (64 shorter events, 32.1 us)
Async XLA Ops:
  7.2 279.1 %copy-start = (bf16[1,512,2,512]{3,2,1,0:T(2,128)(2,1)S(1)}, bf16[1,512,2,512]{3,2,1,0:T(2,128)(2,1)}, u32[]{:S(2)}) copy-start(bf16[1,512,2,512]{3,2,1,0:T(2,128)(2,1)} %param.15) | copy-start | bytes 3145732
  7.2 105.5 %all-gather.6.cloned.1.call-start = ((), (), s32[]{:S(2)}) async-start(), calls=%async_computation.1 | async-start | bytes 8650752 | tf_op jit(solution)/shard_map/all_gather | solution.py:14
  9.1 263.6 %all-gather.8.cloned.1.call-start = ((), (), s32[]{:S(2)}) async-start(), calls=%async_computation.2 | async-start | bytes 2359296 | tf_op jit(solution)/shard_map/all_gather | solution.py:72
  112.8 0.7 copy-start.2
  112.8 1.6 copy-start.4
  114.3 254.7 %reduce-scatter.2.cloned.1.call-start = ((), (), s32[]{:S(2)}) async-start(), calls=%async_computation.3 | async-start | bytes 2359296 | tf_op jit(solution)/shard_map/reduce_scatter | solution.py:76
  118.6 167.5 %copy-start.3 = (f32[2,2,128]{2,1,0:T(2,128)S(1)}, f32[2,2,128]{2,1,0:T(2,128)}, u32[]{:S(2)}) copy-start(f32[2,2,128]{2,1,0:T(2,128)} %param.16) | copy-start | bytes 6148
  118.6 167.7 %copy-start.1 = (bf16[512,2,128]{0,2,1:T(8,128)(2,1)S(1)}, bf16[512,2,128]{0,2,1:T(8,128)(2,1)}, u32[]{:S(2)}) copy-start(bf16[512,2,128]{0,2,1:T(8,128)(2,1)} %fusion.19) | copy-start | bytes 786436
  286.0 188.7 %all-gather.10.cloned.1.call-start = ((), (), s32[]{:S(2)}) async-start(), calls=%async_computation.4 | async-start | bytes 8650752 | tf_op jit(solution)/shard_map/all_gather | solution.py:14
Sparse Core Ops, SparseCore 0:
  11.2 101.4 all-gather.5
  115.0 157.6 all-gather.7
  286.1 34.6 reduce-scatter.1
  371.3 103.2 all-gather.9
where the time goes:
time: 598 us; the launch traced here: 596 us
  waiting for transfers between devices  303 us (51%)
  blocking collectives  131 us (22%)
  other arithmetic  92.9 us (16%)
  local copies, waits for them, and re-layouts  31.4 us (5%)
  matrix products  22.2 us (4%)
  between operations  14 us (2%)
    all_gather x1, waiting for transfers between devices, on_device(): lax.all_gather(forward_b, 'space', axis=0, tiled=True)  154 us
    all_gather x2, waiting for transfers between devices, carried_in(): lax.all_gather(a.astype(kind), axis)  149 us
    psum x1, blocking collectives, on_device(): fixed_forward = lax.psum(contrib, ('tm', 'space')).astype(jnp.bfloat16)  78.9 us
    add x31, other arithmetic, combine(): value_l + latter[0] * value_e  62.3 us
    all_gather x1, blocking collectives, carried_in(): lax.all_gather(a.astype(kind), axis)  52.1 us
    convert_element_type x31, other arithmetic, one(): lax.dynamic_index_in_dim(a, source, 0, False).astype(own.dtype)  28.8 us
    while x4, local copies, waits for them, and re-layouts, carried_in(): return lax.fori_loop(0, ahead, one, state)  24.8 us
    dot_general x1, matrix products, on_device(): jnp.einsum('hrn,rhk->nhk', block, inner_rows, preferred_element_type=jnp....  13.2 us
  transfers between devices with their start and end apart: 4, of which 3 were waited for; matrix products, arithmetic and copies ran while one was open for 2% of the time, Pallas kernels for 0%

commit v1 on v0

--- a/solution.py
+++ b/solution.py
@@ -88,7 +88,7 @@
     contrib = -coupling
     own_part = lax.dynamic_slice_in_dim(contrib, share_start, share_rows, 1) + fixed_rhs
     contrib = lax.dynamic_update_slice_in_dim(contrib, own_part, share_start, 1)
-    fixed_forward = lax.psum(contrib, ("tm", "space")).astype(jnp.bfloat16)
+    fixed_forward = jnp.sum(lax.all_gather(contrib, ("tm", "space")), axis=0).astype(jnp.bfloat16)
     fixed_total = tip_factor.shape[1]
     fixed_index = jnp.arange(fixed_total, dtype=jnp.int32)
     lower_tri = fixed_index[:, None] >= fixed_index[None, :]

time: 598 us -> 895 us (1.50)
  waiting for transfers between devices: 303 us -> 636 us
  blocking collectives: 131 us -> 52.1 us
  other arithmetic: 92.9 us -> 134 us
    all_gather x0 -> x1, waiting for transfers between devices: none -> 338 us  [on_device(): lax.all_gather(contrib, ('tm', 'space'))]
    psum x1 -> x0, blocking collectives: 78.9 us -> none  [on_device(): fixed_forward = lax.psum(contrib, ('tm', 'space')).astype(jnp.bfloat16)]
    reduce_sum x0 -> x1, other arithmetic: none -> 41.4 us  [on_device(): jnp.sum(lax.all_gather(contrib, ('tm', 'space')), axis=0)]
  transfers between devices with their start and end apart: 4 -> 5, of which waited for: 3 -> 4; matrix products, arithmetic and copies ran while one was open for 2% -> 8% of each run, Pallas kernels for 0% -> 0%
where the time goes in v1:
time: 895 us; the launch traced here: 893 us
  waiting for transfers between devices  636 us (71%)
  other arithmetic  134 us (15%)
  blocking collectives  52.1 us (6%)
  local copies, waits for them, and re-layouts  32.2 us (4%)
  matrix products  23.5 us (3%)
  between operations  14 us (2%)
    all_gather x1, waiting for transfers between devices, on_device(): lax.all_gather(contrib, ('tm', 'space'))  338 us
    all_gather x1, waiting for transfers between devices, on_device(): lax.all_gather(forward_b, 'space', axis=0, tiled=True)  151 us
    all_gather x2, waiting for transfers between devices, carried_in(): lax.all_gather(a.astype(kind), axis)  147 us
    add x31, other arithmetic, combine(): value_l + latter[0] * value_e  62.3 us
    all_gather x1, blocking collectives, carried_in(): lax.all_gather(a.astype(kind), axis)  52.1 us
    reduce_sum x1, other arithmetic, on_device(): jnp.sum(lax.all_gather(contrib, ('tm', 'space')), axis=0)  41.4 us
    convert_element_type x31, other arithmetic, one(): lax.dynamic_index_in_dim(a, source, 0, False).astype(own.dtype)  28.7 us
    while x4, local copies, waits for them, and re-layouts, carried_in(): return lax.fori_loop(0, ahead, one, state)  24.8 us
  transfers between devices with their start and end apart: 5, of which 4 were waited for; matrix products, arithmetic and copies ran while one was open for 8% of the time, Pallas kernels for 0%

profile of v1, /device:TPU:2, one launch (start us, length us, event | category | flops | bytes accessed | tf_op | source)
XLA Modules:
  0.0 892.9 jit_solution(9895036819756672031)
XLA Ops:
  7.2 1.9 copy.67
  9.2 1.2 copy.36
  11.1 52.1 %all-gather = bf16[32,512,2]{1,2,0:T(2,128)(2,1)S(1)} all-gather(bf16[1,512,2]{1,2,0:T(2,128)(2,1)S(1)} %convert_element_type.103), channel_id=2, replica_groups=mesh['tm'=32,'space'=8] {'tm'}, dimensions={0}, use_global_device_ids=true | all-gather | bytes 67584 | tf_op jit(solution)/shard_map/all_gather | solution.py:14
  63.2 3.3 copy.39
  66.6 46.0 %all-gather.7.cloned.1.call-done = bf16[32,512,2,128]{3,1,2,0:T(8,128)(2,1)} async-done(((bf16[1,512,2,128]{3,1,2,0:T(8,128)(2,1)}), bf16[32,512,2,128]{3,1,2,0:T(8,128)(2,1)}) %all-gather.7.cloned.1.call-update) | async-done | bytes 8388624 | tf_op jit(solution)/shard_map/all_gather | solution.py:14
  114.1 1.3 convolution_negate_fusion
  115.5 1.1 dynamic_update_slice.4
  117.7 4.1 fusion
  121.8 150.9 %all-gather.9.cloned.1.call-done = bf16[4096,2,128]{0,2,1:T(8,128)(2,1)} async-done(((bf16[512,2,128]{0,2,1:T(8,128)(2,1)}), bf16[4096,2,128]{0,2,1:T(8,128)(2,1)}) %all-gather.9.cloned.1.call-update) | async-done | bytes 2097168 | tf_op jit(solution)/shard_map/all_gather | solution.py:72
  272.7 13.6 %fusion.4 = bf16[4096,2,128]{0,2,1:T(8,128)(2,1)} fusion(bf16[2,1,512,4096]{3,2,1,0:T(8,128)(2,1)} %param.11, pred[512,4096]{1,0:T(8,128)(4,1)} %fusion, bf16[4096,2,128]{0,2,1:T(8,128)(2,1)} %all-gather.9.cloned.1.call-done), kind=kOutput, calls=%fused_computation.12 | convolution fusion | flops 2157051904 | bytes 14680064 | tf_op jit(solution)/shard_map/hrn,rhk->nhk/dot_general | solution.py:77
  286.5 337.8 %all-gather.11.cloned.1.call-done = f32[256,2,512,128]{3,2,1,0:T(8,128)} async-done(((f32[1,2,512,128]{3,2,1,0:T(8,128)}), f32[256,2,512,128]{3,2,1,0:T(8,128)}) %all-gather.11.cloned.1.call-update) | async-done | bytes 134217744 | tf_op jit(solution)/shard_map/all_gather | solution.py:91
  624.3 41.4 %reduce_sum.9 = bf16[2,512,128]{2,1,0:T(8,128)(2,1)S(1)} reduce(f32[256,2,512,128]{3,2,1,0:T(8,128)} %all-gather.11.cloned.1.call-done, f32[]{:T(128)} %constant.87.clone.1), dimensions={0}, to_apply=%region_3.4 | reduce | flops 33423360 | bytes 134479872 | tf_op jit(solution)/shard_map/reduce_sum | solution.py:91
  665.9 2.4 fusion.9
  668.3 2.1 multiply_convert_fusion
  671.0 100.6 %all-gather.13.cloned.1.call-done = bf16[16384,2,128]{0,2,1:T(8,128)(2,1)} async-done(((bf16[512,2,128]{0,2,1:T(8,128)(2,1)}), bf16[16384,2,128]{0,2,1:T(8,128)(2,1)}) %all-gather.13.cloned.1.call-update) | async-done | bytes 8388624 | tf_op jit(solution)/shard_map/all_gather | solution.py:14
  771.7 21.1 %copy.56 = bf16[16384,2,128]{2,1,0:T(2,128)(2,1)} copy(bf16[16384,2,128]{0,2,1:T(8,128)(2,1)} %all-gather.13.cloned.1.call-done) | data formatting | bytes 16777216 | tf_op jit(solution)/shard_map/while | solution.py:29
  792.9 92.2 %while.27 = (s32[]{:T(128)}, f32[512,2,128]{2,1,0:T(2,128)S(1)}, s32[]{:T(128)}, bf16[32,512,2,128]{3,2,1,0:T(2,128)(2,1)}, bf16[32,512,2,1]{2,1,3,0:T(8,128)(2,...) while((s32[]{:T(128)}, f32[512,2,128]{2,1,0:T(2,128)S(1)}, s32[]{:T(128)}, ...), condition=%wide.region_5.6_spmd, body=%wide.region_4.5_spmd.sunk | while | flops 394246 | bytes 1321107 | solution.py:29
  793.8 2.0 convert_add_fusion.5
  796.8 2.0 convert_add_fusion.5
  799.8 2.0 convert_add_fusion.5
  802.8 2.0 convert_add_fusion.5
  805.7 2.0 convert_add_fusion.5
  808.7 2.0 convert_add_fusion.5
  811.7 2.0 convert_add_fusion.5
  814.6 2.0 convert_add_fusion.5
  817.6 2.0 convert_add_fusion.5
  820.6 2.0 convert_add_fusion.5
  823.6 2.0 convert_add_fusion.5
  826.5 2.0 convert_add_fusion.5
  829.5 2.0 convert_add_fusion.5
  832.5 2.0 convert_add_fusion.5
  835.5 2.0 convert_add_fusion.5
  838.4 2.0 convert_add_fusion.5
  841.4 2.0 convert_add_fusion.5
  844.4 2.0 convert_add_fusion.5
  847.3 2.0 convert_add_fusion.5
  850.3 2.0 convert_add_fusion.5
  853.3 2.0 convert_add_fusion.5
  856.3 2.0 convert_add_fusion.5
  859.2 2.0 convert_add_fusion.5
  862.2 2.0 convert_add_fusion.5
  865.2 2.0 convert_add_fusion.5
  868.1 2.0 convert_add_fusion.5
  871.1 2.0 convert_add_fusion.5
  874.1 2.0 convert_add_fusion.5
  877.1 2.0 convert_add_fusion.5
  880.0 2.0 convert_add_fusion.5
  883.0 2.0 convert_add_fusion.5
  (67 shorter events, 34.4 us)
Async XLA Ops:
  7.2 106.9 %copy-start = (bf16[1,512,2,512]{3,2,1,0:T(2,128)(2,1)S(1)}, bf16[1,512,2,512]{3,2,1,0:T(2,128)(2,1)}, u32[]{:S(2)}) copy-start(bf16[1,512,2,512]{3,2,1,0:T(2,128)(2,1)} %param.15) | copy-start | bytes 3145732
  7.2 105.5 %all-gather.7.cloned.1.call-start = ((), (), s32[]{:S(2)}) async-start(), calls=%async_computation.1 | async-start | bytes 8650752 | tf_op jit(solution)/shard_map/all_gather | solution.py:14
  9.1 263.6 %all-gather.9.cloned.1.call-start = ((), (), s32[]{:S(2)}) async-start(), calls=%async_computation.2 | async-start | bytes 2359296 | tf_op jit(solution)/shard_map/all_gather | solution.py:72
  63.2 49.8 %copy-start.1 = (f32[1,512,2]{1,2,0:T(2,128)S(1)}, f32[1,512,2]{1,2,0:T(2,128)}, u32[]{:S(2)}) copy-start(f32[1,512,2]{1,2,0:T(2,128)} %param.13) | copy-start | bytes 12292
  66.6 47.3 %copy-start.2 = (f32[2,2,128]{2,1,0:T(2,128)S(1)}, f32[2,2,128]{2,1,0:T(2,128)}, u32[]{:S(2)}) copy-start(f32[2,2,128]{2,1,0:T(2,128)} %param.16) | copy-start | bytes 6148
  112.8 4.9 copy-start.3
  113.9 510.5 %all-gather.11.cloned.1.call-start = ((), (), s32[]{:S(2)}) async-start(), calls=%async_computation.4 | async-start | bytes 134742016 | tf_op jit(solution)/shard_map/all_gather | solution.py:91
  117.6 550.7 %reduce-scatter.2.cloned.1.call-start = ((), (), s32[]{:S(2)}) async-start(), calls=%async_computation.3 | async-start | bytes 2359296 | tf_op jit(solution)/shard_map/reduce_scatter | solution.py:76
  286.3 485.3 %all-gather.13.cloned.1.call-start = ((), (), s32[]{:S(2)}) async-start(), calls=%async_computation.5 | async-start | bytes 8650752 | tf_op jit(solution)/shard_map/all_gather | solution.py:14
Sparse Core Ops, SparseCore 0:
  11.2 101.4 all-gather.6
  114.5 158.2 all-gather.8
  277.0 347.2 all-gather.10
  626.7 30.2 reduce-scatter.1
  670.6 101.0 all-gather.12
